TPU v7x, 32 devices: a whole 2x2x4 slice. The times are simulated.
32 devices in a mesh: seq: 16 (over z, x, core), tp: 2 (over y).
Axes of the slice: x: 2, y: 2, z: 4, core: 2. Of those that a mesh axis runs over, the one named last changes fastest.
Arguments:
- tokens: bfloat16 [2048, 5120], P('seq', 'tp'), may hold values from -4 to 4
- self_queries: bfloat16 [2048, 3072], P('seq', 'tp'), may hold values from -12 to 12
- self_keys: bfloat16 [2048, 3072], P('seq', 'tp'), may hold values from -12 to 12
- self_values: bfloat16 [2048, 3072], P('seq', 'tp'), may hold values from -6 to 6
- cross_queries: bfloat16 [2048, 3072], P('seq', 'tp'), may hold values from -12 to 12
- caption_keys: bfloat16 [512, 3072], P('seq', 'tp'), may hold values from -12 to 12
- caption_values: bfloat16 [512, 3072], P('seq', 'tp'), may hold values from -6 to 6
- out_weight: bfloat16 [3072, 5120], P('tp'), may hold values from -0.15625 to 0.15625
- gate_vector: float32 [5120], P('tp'), may hold values from -6 to 6
Outputs:
- updated: bfloat16 [2048, 5120], P('seq', 'tp')
- cross_heads: bfloat16 [2048, 3072], P('seq', 'tp')
All inputs are finite; a program needn't handle non-finite values.
Results may differ from a plain program's by a relative error of at most 0.0085.
Values may be sent and summed in bfloat16 or wider, within the bound.
No kernel may reach another device: no remote copies, remote signals or barrier semaphores. Data moves between devices by JAX's collectives and lax.ppermute only.
A program may use at most 128 MiB of HBM per device.

v0:
```python
import math
import jax
import jax.numpy as jnp
from jax import lax
from jax.sharding import PartitionSpec as P

DH = 128


def online_step(running, pieces, query_split, score_scale):
    maxima, totals, accum = running
    keys_piece, values_piece = pieces
    row_count = keys_piece.shape[0]
    heads_here = query_split.shape[1]
    keys_split = keys_piece.reshape(row_count, heads_here, DH)
    values_split = values_piece.reshape(row_count, heads_here, DH)
    scores = (
        jnp.einsum("thd,khd->thk", query_split, keys_split, preferred_element_type=jnp.float32)
        * score_scale
    )
    new_max = jnp.maximum(maxima, jnp.max(scores, axis=2))
    rescale = jnp.exp(maxima - new_max)
    exp_scores = jnp.exp(scores - new_max[:, :, None])
    totals = totals * rescale + jnp.sum(exp_scores, axis=2)
    weights = exp_scores.astype(jnp.bfloat16)
    accum = accum * rescale[:, :, None] + jnp.einsum(
        "thk,khd->thd", weights, values_split, preferred_element_type=jnp.float32
    )
    return (new_max, totals, accum)


def bounded_step(running, pieces, query_split, score_scale):
    row_count = pieces[0].shape[0]
    block_rows = math.gcd(row_count, 1024)
    if block_rows == row_count:
        return online_step(running, pieces, query_split, score_scale)

    def loop_body(position, current):
        keys_piece = lax.dynamic_slice_in_dim(pieces[0], position * block_rows, block_rows, 0)
        values_piece = lax.dynamic_slice_in_dim(pieces[1], position * block_rows, block_rows, 0)
        return online_step(current, (keys_piece, values_piece), query_split, score_scale)

    return lax.fori_loop(0, row_count // block_rows, loop_body, running)


def initial_state(row_count, heads_here):
    return (
        jnp.full((row_count, heads_here), -1e30, jnp.float32),
        jnp.zeros((row_count, heads_here), jnp.float32),
        jnp.zeros((row_count, heads_here, DH), jnp.float32),
    )


def finish(running):
    maxima, totals, accum = running
    row_count, heads_here = totals.shape
    return (accum / totals[:, :, None]).reshape(row_count, heads_here * DH).astype(jnp.bfloat16)


def shards(
    tokens,
    self_queries,
    self_keys,
    self_values,
    cross_queries,
    caption_keys,
    caption_values,
    out_weight,
    gate_vector,
):
    row_count = self_queries.shape[0]
    heads_here = self_queries.shape[1] // DH
    score_scale = 1.0 / math.sqrt(DH)
    self_split = self_queries.reshape(row_count, heads_here, DH)
    cross_split = cross_queries.reshape(row_count, heads_here, DH)
    self_state = bounded_step(
        initial_state(row_count, heads_here),
        (
            lax.all_gather(self_keys, "seq", axis=0, tiled=True),
            lax.all_gather(self_values, "seq", axis=0, tiled=True),
        ),
        self_split,
        score_scale,
    )
    self_heads = finish(self_state)
    caption_all = (
        lax.all_gather(caption_keys, "seq", axis=0, tiled=True),
        lax.all_gather(caption_values, "seq", axis=0, tiled=True),
    )
    cross_state = bounded_step(
        initial_state(row_count, heads_here), caption_all, cross_split, score_scale
    )
    cross_heads = finish(cross_state)
    partial_terms = jnp.dot(self_heads, out_weight, preferred_element_type=jnp.float32)
    projected = lax.psum_scatter(
        partial_terms.astype(jnp.bfloat16), "tp", scatter_dimension=1, tiled=True
    ).astype(jnp.float32)
    updated = (tokens.astype(jnp.float32) + gate_vector[None, :] * projected).astype(jnp.bfloat16)
    return (updated, cross_heads)


def solution(mesh):
    return jax.shard_map(
        shards,
        mesh=mesh,
        in_specs=(
            P("seq", "tp"),
            P("seq", "tp"),
            P("seq", "tp"),
            P("seq", "tp"),
            P("seq", "tp"),
            P("seq", "tp"),
            P("seq", "tp"),
            P("tp", None),
            P("tp"),
        ),
        out_specs=(P("seq", "tp"), P("seq", "tp")),
        check_vma=False,
    )
```

profile of v0, /device:TPU:0, one launch (start us, length us, event | category | flops | bytes accessed | tf_op | source)
XLA Modules:
  0.0 259.5 jit_solution(5244744670284265529)
XLA Ops:
  7.2 1.9 copy.32
  9.2 1.9 copy.34
  12.5 1.2 copy.33
  14.0 65.1 %all-gather.5.cloned.1.call-done = bf16[2048,1536]{0,1:T(8,128)(2,1)} async-done(((bf16[128,1536]{0,1:T(8,128)(2,1)}), bf16[2048,1536]{0,1:T(8,128)(2,1)}) %all-gather.5.cloned.1.call-update) | async-done | bytes 6291472 | tf_op jit(solution)/shard_map/all_gather | solution.py:79
  79.1 66.6 %all-gather.7.cloned.1.call-done = bf16[2048,1536]{0,1:T(8,128)(2,1)} async-done(((bf16[128,1536]{0,1:T(8,128)(2,1)}), bf16[2048,1536]{0,1:T(8,128)(2,1)}) %all-gather.7.cloned.1.call-update) | async-done | bytes 6291472 | tf_op jit(solution)/shard_map/all_gather | solution.py:80
  145.7 30.5 %while.18 = (s32[]{:T(128)}, f32[128,12]{0,1:T(8,128)S(1)}, f32[128,12]{0,1:T(8,128)}, f32[128,12,128]{0,2,1:T(8,128)}, bf16[2048,1536]{0,1:T(8,128)(2,1)}, /*in...) while((s32[]{:T(128)}, f32[128,12]{0,1:T(8,128)S(1)}, ...), condition=%wide.region_3.0_spmd.clone, body=%wide.region_0.0_spmd.clone.sunk | while | flops 818486784 | bytes 65028356 | solution.py:43
  145.7 3.6 %constant_dynamic-slice_fusion.3 = (bf16[1024,1536]{0,1:T(8,128)(2,1)S(1)}, bf16[1024,1536]{0,1:T(8,128)(2,1)S(1)}) fusion(bf16[2048,1536]{0,1:T(8,128)(2,1)} %get-tuple-element.280, s32[]{:T(128)S(6)} %select_n.10, bf16[2048,1536]{0,1:T(8,128)(2,1)} %get-tuple-element.278), kind=kLoop, calls=%fused_computation.15.clone.1 | loop fusion | bytes 12582916 | tf_op jit(solution)/shard_map/while/body/eval_jaxpr/dynamic_slice | solution.py:40
  149.3 3.8 %bitcast_reduce_fusion.3 = (f32[128,12]{0,1:T(8,128)S(1)}, f32[12,1024,128]{2,1,0:T(8,128)}) fusion(bf16[1024,12,128]{0,2,1:T(8,128)(2,1)S(1)} %bitcast.79, bf16[128,12,128]{2,0,1:T(8,128)(2,1)S(1)} %get-tuple-element.279), kind=kOutput, calls=%fused_computation.1.clone.1 | convolution fusion | flops 405797376 | bytes 9836544 | tf_op jit(solution)/shard_map/while/body/eval_jaxpr/thd,khd->thk/dot_general | solution.py:18
  153.1 4.0 %fusion.55 = f32[128,12]{0,1:T(8,128)S(1)} fusion(f32[12,1024,128]{2,1,0:T(8,128)} %get-tuple-element.248, f32[128,12]{0,1:T(8,128)S(1)} %select_maximum_fusion.2), kind=kLoop, calls=%fused_computation.4.clone.1 | loop fusion | flops 4717056 | bytes 6303744 | tf_op jit(solution)/shard_map/while/body/eval_jaxpr/reduce_sum | solution.py:24
  157.8 2.5 fusion.57
  160.4 3.6 %constant_dynamic-slice_fusion.3 = (bf16[1024,1536]{0,1:T(8,128)(2,1)S(1)}, bf16[1024,1536]{0,1:T(8,128)(2,1)S(1)}) fusion(bf16[2048,1536]{0,1:T(8,128)(2,1)} %get-tuple-element.280, s32[]{:T(128)S(6)} %select_n.10, bf16[2048,1536]{0,1:T(8,128)(2,1)} %get-tuple-element.278), kind=kLoop, calls=%fused_computation.15.clone.1 | loop fusion | bytes 12582916 | tf_op jit(solution)/shard_map/while/body/eval_jaxpr/dynamic_slice | solution.py:40
  163.9 3.8 %bitcast_reduce_fusion.3 = (f32[128,12]{0,1:T(8,128)S(1)}, f32[12,1024,128]{2,1,0:T(8,128)}) fusion(bf16[1024,12,128]{0,2,1:T(8,128)(2,1)S(1)} %bitcast.79, bf16[128,12,128]{2,0,1:T(8,128)(2,1)S(1)} %get-tuple-element.279), kind=kOutput, calls=%fused_computation.1.clone.1 | convolution fusion | flops 405797376 | bytes 9836544 | tf_op jit(solution)/shard_map/while/body/eval_jaxpr/thd,khd->thk/dot_general | solution.py:18
  167.8 4.0 %fusion.55 = f32[128,12]{0,1:T(8,128)S(1)} fusion(f32[12,1024,128]{2,1,0:T(8,128)} %get-tuple-element.248, f32[128,12]{0,1:T(8,128)S(1)} %select_maximum_fusion.2), kind=kLoop, calls=%fused_computation.4.clone.1 | loop fusion | flops 4717056 | bytes 6303744 | tf_op jit(solution)/shard_map/while/body/eval_jaxpr/reduce_sum | solution.py:24
  171.8 0.8 copy-done
  172.6 3.7 %fusion.57 = f32[128,12,128]{0,2,1:T(8,128)} fusion(bf16[1024,12,128]{0,2,1:T(8,128)(2,1)S(1)} %bitcast.78, f32[12,1024,128]{2,1,0:T(8,128)S(1)} %copy-done, f32[128,12]{0,1:T(8,128)S(1)} %select_maximum_fusion.2, f32[128,12,128]{0,2,1:T(8,128)} %get-tuple-element.266, f32[128,12]{0,1:T(8,128)S(1)} %get-tuple-element.251, pred[]{:T(512)S(6)} %compare.3), kind=kOutput, calls=%fused_computation.9.clone.1 | convolution fusion | flops 407961600 | bytes 11022337 | tf_op jit(solution)/shard_map/while/body/eval_jaxpr/thk,khd->thd/dot_general | solution.py:26
  176.2 1.2 divide_convert_fusion
  177.5 9.0 %convolution_convert_fusion = bf16[128,5120]{1,0:T(8,128)(2,1)} fusion(bf16[128,1536]{0,1:T(8,128)(2,1)S(1)} %bitcast.81, bf16[1536,5120]{1,0:T(8,128)(2,1)} %param.18), kind=kOutput, calls=%fused_computation.18 | convolution fusion | flops 2013921280 | bytes 17432576 | tf_op jit(solution)/shard_map/dot_general | solution.py:94
  186.8 1.7 copy.40
  188.5 38.1 %all-gather.9.cloned.1.call-done = bf16[512,1536]{1,0:T(8,128)(2,1)} async-done(((bf16[32,1536]{1,0:T(8,128)(2,1)}), bf16[512,1536]{1,0:T(8,128)(2,1)}) %all-gather.9.cloned.1.call-update) | async-done | bytes 1572880 | tf_op jit(solution)/shard_map/all_gather | solution.py:87
  226.6 1.7 copy.36
  229.6 0.9 fusion.31
  230.5 0.9 copy.42
  231.4 19.4 %reduce-scatter.2.cloned.1.call-done = bf16[128,2560]{1,0:T(8,128)(2,1)} async-done(((bf16[128,5120]{1,0:T(8,128)(2,1)}), bf16[128,2560]{1,0:T(8,128)(2,1)}) %reduce-scatter.2.cloned.1.call-update) | async-done | bytes 655376 | tf_op jit(solution)/shard_map/reduce_scatter | solution.py:95
  250.9 2.1 add_convert_fusion
  (43 shorter events, 3.8 us)
Async XLA Ops:
  7.2 72.0 %all-gather.5.cloned.1.call-start = ((), (), s32[]{:S(2)}) async-start(), calls=%async_computation.1 | async-start | bytes 6684672 | tf_op jit(solution)/shard_map/all_gather | solution.py:79
  9.1 136.6 %all-gather.7.cloned.1.call-start = ((), (), s32[]{:S(2)}) async-start(), calls=%async_computation.2 | async-start | bytes 6684672 | tf_op jit(solution)/shard_map/all_gather | solution.py:80
  11.1 175.6 %all-gather.11.cloned.1.call-start = ((), (), s32[]{:S(2)}) async-start(), calls=%async_computation.5 | async-start | bytes 1671168 | tf_op jit(solution)/shard_map/all_gather | solution.py:88
  11.9 214.8 %all-gather.9.cloned.1.call-start = ((), (), s32[]{:S(2)}) async-start(), calls=%async_computation.4 | async-start | bytes 1671168 | tf_op jit(solution)/shard_map/all_gather | solution.py:87
  12.5 238.4 %reduce-scatter.2.cloned.1.call-start = ((), (), s32[]{:S(2)}) async-start(), calls=%async_computation.3 | async-start | bytes 1966080 | tf_op jit(solution)/shard_map/reduce_scatter | solution.py:95
  153.1 4.0 %copy-start.3 = (f32[128,12]{0,1:T(8,128)S(1)}, f32[128,12]{0,1:T(8,128)}, u32[]{:S(2)}) copy-start(f32[128,12]{0,1:T(8,128)} %get-tuple-element.265) | copy-start | bytes 18436 | tf_op jit(solution)/shard_map/while
  153.1 4.7 %copy-start = (f32[12,1024,128]{2,1,0:T(8,128)S(1)}, f32[12,1024,128]{2,1,0:T(8,128)}, u32[]{:S(2)}) copy-start(f32[12,1024,128]{2,1,0:T(8,128)} %get-tuple-element.248) | copy-start | bytes 18874372 | tf_op jit(solution)/shard_map/while
  157.2 3.2 %copy-start.4 = (f32[128,12]{0,1:T(8,128)}, f32[128,12]{0,1:T(8,128)S(1)}, u32[]{:S(2)}) copy-start(f32[128,12]{0,1:T(8,128)S(1)} %get-tuple-element.276) | copy-start | bytes 18436 | tf_op jit(solution)/shard_map/while
  167.8 4.0 %copy-start.3 = (f32[128,12]{0,1:T(8,128)S(1)}, f32[128,12]{0,1:T(8,128)}, u32[]{:S(2)}) copy-start(f32[128,12]{0,1:T(8,128)} %get-tuple-element.265) | copy-start | bytes 18436 | tf_op jit(solution)/shard_map/while
  167.8 4.8 %copy-start = (f32[12,1024,128]{2,1,0:T(8,128)S(1)}, f32[12,1024,128]{2,1,0:T(8,128)}, u32[]{:S(2)}) copy-start(f32[12,1024,128]{2,1,0:T(8,128)} %get-tuple-element.248) | copy-start | bytes 18874372 | tf_op jit(solution)/shard_map/while
  171.8 4.5 %copy-start.4 = (f32[128,12]{0,1:T(8,128)}, f32[128,12]{0,1:T(8,128)S(1)}, u32[]{:S(2)}) copy-start(f32[128,12]{0,1:T(8,128)S(1)} %get-tuple-element.276) | copy-start | bytes 18436 | tf_op jit(solution)/shard_map/while
  177.5 9.0 %copy-start.2 = (bf16[128,1536]{1,0:T(8,128)(2,1)S(1)}, bf16[128,1536]{1,0:T(8,128)(2,1)}, u32[]{:S(2)}) copy-start(bf16[128,1536]{1,0:T(8,128)(2,1)} %param.15) | copy-start | bytes 1179652
  229.6 21.2 %copy-start.1 = (bf16[128,2560]{1,0:T(8,128)(2,1)S(1)}, bf16[128,2560]{1,0:T(8,128)(2,1)}, u32[]{:S(2)}) copy-start(bf16[128,2560]{1,0:T(8,128)(2,1)} %param.11) | copy-start | bytes 1966084
  229.6 21.2 %copy-start.5 = (f32[2560]{0:T(1024)S(1)}, f32[2560]{0:T(1024)}, u32[]{:S(2)}) copy-start(f32[2560]{0:T(1024)} %param.19) | copy-start | bytes 30724
Sparse Core Ops, SparseCore 0:
  10.7 68.3 all-gather.4
  81.9 63.8 all-gather.6
  148.0 37.8 all-gather.10
  188.0 38.5 all-gather.8
  228.7 22.0 reduce-scatter.1
where the time goes:
time: 260 us
  waiting for transfers between devices  191 us (73%)
  matrix products  24.4 us (9%)
  local copies, waits for them, and re-layouts  18.4 us (7%)
  between operations  13.9 us (5%)
  other arithmetic  11.9 us (5%)
    all_gather x1, waiting for transfers between devices, shards(): lax.all_gather(self_values, 'seq', axis=0, tiled=True)  66.6 us
    all_gather x1, waiting for transfers between devices, shards(): lax.all_gather(self_keys, 'seq', axis=0, tiled=True)  65.1 us
    all_gather x1, waiting for transfers between devices, shards(): lax.all_gather(caption_keys, 'seq', axis=0, tiled=True)  38.1 us
    reduce_scatter x1, waiting for transfers between devices, shards(): lax.psum_scatter(partial_terms.astype(jnp.bfloat16), 'tp', scatter_dimens...  19.4 us
    dot_general x1, matrix products, shards(): jnp.dot(self_heads, out_weight, preferred_element_type=jnp.float32)  8.99 us
    reduce_sum x3, other arithmetic, online_step(): totals = totals * rescale + jnp.sum(exp_scores, axis=2)  8.54 us
    dot_general x3, matrix products, online_step(): jnp.einsum('thd,khd->thk', query_split, keys_split, preferred_element_typ...  8.36 us
    dynamic_slice x2, local copies, waits for them, and re-layouts, loop_body(): lax.dynamic_slice_in_dim(pieces[1], position * block_rows, block_rows, 0)  7.11 us
  transfers between devices with their start and end apart: 5, of which 4 were waited for; matrix products, arithmetic and copies ran while one was open for 19% of the time, Pallas kernels for 0%

commit v1 on v0

--- a/solution.py
+++ b/solution.py
@@ -5,6 +5,18 @@
 from jax.sharding import PartitionSpec as P
 
 DH = 128
+
+
+def collect(x, axis, dim):
+    ways, here, step = (lax.axis_size(axis), lax.axis_index(axis), x.shape[dim])
+    line, have = (x, 1)
+    while have < ways:
+        line = jnp.concatenate(
+            [line, lax.ppermute(line, axis, [(d, (d - have) % ways) for d in range(ways)])],
+            axis=dim,
+        )
+        have = 2 * have
+    return jnp.roll(line, here * step, axis=dim)
 
 
 def online_step(running, pieces, query_split, score_scale):
@@ -84,7 +96,7 @@
     )
     self_heads = finish(self_state)
     caption_all = (
-        lax.all_gather(caption_keys, "seq", axis=0, tiled=True),
+        collect(caption_keys, "seq", 0),
         lax.all_gather(caption_values, "seq", axis=0, tiled=True),
     )
     cross_state = bounded_step(

time: 260 us -> 265 us (1.019)
  waiting for transfers between devices: 191 us -> 173 us
  starting transfers between devices: 0.2 us -> 9.23 us
  local copies, waits for them, and re-layouts: 18.4 us -> 25.8 us
  other arithmetic: 11.9 us -> 15.7 us
    ppermute x0 -> x4, waiting for transfers between devices: none -> 52.7 us  [collect(): lax.ppermute(line, axis, [(d, (d - have) % ways) for d in range(ways)])]
    all_gather x1 -> x0, waiting for transfers between devices: 38.1 us -> none  [shards(): lax.all_gather(caption_keys, 'seq', axis=0, tiled=True)]
    reduce_scatter x1, waiting for transfers between devices: 19.4 us -> 0.01 us  [shards(): lax.psum_scatter(partial_terms.astype(jnp.bfloat16), 'tp', scatter_dimens...]
    all_gather x1, waiting for transfers between devices: 65.1 us -> 53.9 us  [shards(): lax.all_gather(self_keys, 'seq', axis=0, tiled=True)]
    ppermute x0 -> x4, starting transfers between devices: none -> 9.07 us  [collect(): lax.ppermute(line, axis, [(d, (d - have) % ways) for d in range(ways)])]
    concatenate x0 -> x1, local copies, waits for them, and re-layouts: none -> 5.89 us  [collect(): return jnp.roll(line, here * step, axis=dim)]
    concatenate x0 -> x3, other arithmetic: none -> 3.01 us  [collect(): jnp.concatenate([line, lax.ppermute(line, axis, [(d, (d - have) % ways) f...]
    unnamed x12 -> x23, local copies, waits for them, and re-layouts: 6.44 us -> 6.62 us
  transfers between devices with their start and end apart: 5 -> 8, of which waited for: 4 -> 5; matrix products, arithmetic and copies ran while one was open for 19% -> 23% of each run, Pallas kernels for 0% -> 0%
where the time goes in v1:
time: 265 us; the launch traced here: 264 us
  waiting for transfers between devices  173 us (65%)
  local copies, waits for them, and re-layouts  25.8 us (10%)
  matrix products  25.8 us (10%)
  other arithmetic  15.7 us (6%)
  between operations  14 us (5%)
  starting transfers between devices  9.23 us (3%)
    all_gather x1, waiting for transfers between devices, shards(): lax.all_gather(self_values, 'seq', axis=0, tiled=True)  66.6 us
    all_gather x1, waiting for transfers between devices, shards(): lax.all_gather(self_keys, 'seq', axis=0, tiled=True)  53.9 us
    ppermute x4, waiting for transfers between devices, collect(): lax.ppermute(line, axis, [(d, (d - have) % ways) for d in range(ways)])  52.7 us
    ppermute x4, starting transfers between devices, collect(): lax.ppermute(line, axis, [(d, (d - have) % ways) for d in range(ways)])  9.07 us
    dot_general x1, matrix products, shards(): jnp.dot(self_heads, out_weight, preferred_element_type=jnp.float32)  9.01 us
    reduce_sum x3, other arithmetic, online_step(): totals = totals * rescale + jnp.sum(exp_scores, axis=2)  8.52 us
    dot_general x3, matrix products, online_step(): jnp.einsum('thk,khd->thd', weights, values_split, preferred_element_type=...  8.44 us
    dot_general x3, matrix products, online_step(): jnp.einsum('thd,khd->thk', query_split, keys_split, preferred_element_typ...  8.39 us
  transfers between devices with their start and end apart: 8, of which 5 were waited for; matrix products, arithmetic and copies ran while one was open for 23% of the time, Pallas kernels for 0%

profile of v1, /device:TPU:0, one launch (start us, length us, event | category | flops | bytes accessed | tf_op | source)
XLA Modules:
  0.0 263.9 jit_solution(9606974078511208315)
XLA Ops:
  7.2 2.0 copy.19
  9.2 1.9 copy.21
  12.4 5.5 %collective-permute-start = (bf16[32,1536]{0,1:T(8,128)(2,1)S(1)}, bf16[32,1536]{0,1:T(8,128)(2,1)S(1)}, u32[]{:S(2)}, u32[]{:S(2)}) collective-permute-start(bf16[32,1536]{0,1:T(8,128)(2,1)S(1)} %copy.27), channel_id=1, source_target_pairs={{0,30},{2,0},{4,2},{6,4},{8,6},{10,8},{12,10},{14,12},{16,14},{18,... | collective-permute-start | bytes 294920 | tf_op jit(solution)/shard_map/ppermute | solution.py:15
  17.8 7.0 %collective-permute-done = bf16[32,1536]{0,1:T(8,128)(2,1)S(1)} collective-permute-done((bf16[32,1536]{0,1:T(8,128)(2,1)S(1)}, bf16[32,1536]{0,1:T(8,128)(2,1)S(1)}, u32[]{:S(2)}, u32[]{:S(2)}) %collective-permute-start) | collective-permute-done | bytes 98336 | tf_op jit(solution)/shard_map/ppermute | solution.py:15
  25.7 11.1 %collective-permute-done.1 = bf16[64,1536]{0,1:T(8,128)(2,1)S(1)} collective-permute-done((bf16[64,1536]{0,1:T(8,128)(2,1)S(1)}, bf16[64,1536]{0,1:T(8,128)(2,1)S(1)}, u32[]{:S(2)}, u32[]{:S(2)}) %collective-permute-start.1) | collective-permute-done | bytes 196640 | tf_op jit(solution)/shard_map/ppermute | solution.py:15
  37.9 1.9 collective-permute-start.2
  39.8 53.9 %all-gather.4.cloned.1.call-done = bf16[2048,1536]{0,1:T(8,128)(2,1)} async-done(((bf16[128,1536]{0,1:T(8,128)(2,1)}), bf16[2048,1536]{0,1:T(8,128)(2,1)}) %all-gather.4.cloned.1.call-update) | async-done | bytes 6291472 | tf_op jit(solution)/shard_map/all_gather | solution.py:91
  93.8 66.6 %all-gather.6.cloned.1.call-done = bf16[2048,1536]{0,1:T(8,128)(2,1)} async-done(((bf16[128,1536]{0,1:T(8,128)(2,1)}), bf16[2048,1536]{0,1:T(8,128)(2,1)}) %all-gather.6.cloned.1.call-update) | async-done | bytes 6291472 | tf_op jit(solution)/shard_map/all_gather | solution.py:92
  160.4 30.4 %while.18 = (s32[]{:T(128)}, f32[128,12]{0,1:T(8,128)S(1)}, f32[128,12]{0,1:T(8,128)}, f32[128,12,128]{0,2,1:T(8,128)}, bf16[2048,1536]{0,1:T(8,128)(2,1)}, /*in...) while((s32[]{:T(128)}, f32[128,12]{0,1:T(8,128)S(1)}, ...), condition=%wide.region_3.0_spmd.clone, body=%wide.region_0.0_spmd.clone.sunk | while | flops 818486784 | bytes 65028356 | solution.py:55
  160.4 3.6 %constant_dynamic-slice_fusion.4 = (bf16[1024,1536]{0,1:T(8,128)(2,1)S(1)}, bf16[1024,1536]{0,1:T(8,128)(2,1)S(1)}) fusion(bf16[2048,1536]{0,1:T(8,128)(2,1)} %get-tuple-element.271, s32[]{:T(128)S(6)} %select_n.25, bf16[2048,1536]{0,1:T(8,128)(2,1)} %get-tuple-element.269), kind=kLoop, calls=%fused_computation.15.clone.1 | loop fusion | bytes 12582916 | tf_op jit(solution)/shard_map/while/body/eval_jaxpr/dynamic_slice | solution.py:52
  163.9 3.8 %bitcast_reduce_fusion.3 = (f32[128,12]{0,1:T(8,128)S(1)}, f32[12,1024,128]{2,1,0:T(8,128)}) fusion(bf16[1024,12,128]{0,2,1:T(8,128)(2,1)S(1)} %bitcast.79, bf16[128,12,128]{2,0,1:T(8,128)(2,1)S(1)} %get-tuple-element.270), kind=kOutput, calls=%fused_computation.1.clone.1 | convolution fusion | flops 405797376 | bytes 9836544 | tf_op jit(solution)/shard_map/while/body/eval_jaxpr/thd,khd->thk/dot_general | solution.py:30
  167.8 4.0 %fusion.55 = f32[128,12]{0,1:T(8,128)S(1)} fusion(f32[12,1024,128]{2,1,0:T(8,128)} %get-tuple-element.239, f32[128,12]{0,1:T(8,128)S(1)} %select_maximum_fusion.2), kind=kLoop, calls=%fused_computation.4.clone.1 | loop fusion | flops 4717056 | bytes 6303744 | tf_op jit(solution)/shard_map/while/body/eval_jaxpr/reduce_sum | solution.py:36
  172.5 2.5 fusion.57
  175.0 3.6 %constant_dynamic-slice_fusion.4 = (bf16[1024,1536]{0,1:T(8,128)(2,1)S(1)}, bf16[1024,1536]{0,1:T(8,128)(2,1)S(1)}) fusion(bf16[2048,1536]{0,1:T(8,128)(2,1)} %get-tuple-element.271, s32[]{:T(128)S(6)} %select_n.25, bf16[2048,1536]{0,1:T(8,128)(2,1)} %get-tuple-element.269), kind=kLoop, calls=%fused_computation.15.clone.1 | loop fusion | bytes 12582916 | tf_op jit(solution)/shard_map/while/body/eval_jaxpr/dynamic_slice | solution.py:52
  178.5 3.8 %bitcast_reduce_fusion.3 = (f32[128,12]{0,1:T(8,128)S(1)}, f32[12,1024,128]{2,1,0:T(8,128)}) fusion(bf16[1024,12,128]{0,2,1:T(8,128)(2,1)S(1)} %bitcast.79, bf16[128,12,128]{2,0,1:T(8,128)(2,1)S(1)} %get-tuple-element.270), kind=kOutput, calls=%fused_computation.1.clone.1 | convolution fusion | flops 405797376 | bytes 9836544 | tf_op jit(solution)/shard_map/while/body/eval_jaxpr/thd,khd->thk/dot_general | solution.py:30
  182.4 4.0 %fusion.55 = f32[128,12]{0,1:T(8,128)S(1)} fusion(f32[12,1024,128]{2,1,0:T(8,128)} %get-tuple-element.239, f32[128,12]{0,1:T(8,128)S(1)} %select_maximum_fusion.2), kind=kLoop, calls=%fused_computation.4.clone.1 | loop fusion | flops 4717056 | bytes 6303744 | tf_op jit(solution)/shard_map/while/body/eval_jaxpr/reduce_sum | solution.py:36
  187.2 3.6 %fusion.57 = f32[128,12,128]{0,2,1:T(8,128)} fusion(bf16[1024,12,128]{0,2,1:T(8,128)(2,1)S(1)} %bitcast.78, f32[12,1024,128]{2,1,0:T(8,128)S(1)} %copy-done, f32[128,12]{0,1:T(8,128)S(1)} %select_maximum_fusion.2, f32[128,12,128]{0,2,1:T(8,128)} %get-tuple-element.257, f32[128,12]{0,1:T(8,128)S(1)} %get-tuple-element.242, pred[]{:T(512)S(6)} %compare.4), kind=kOutput, calls=%fused_computation.9.clone.1 | convolution fusion | flops 407961600 | bytes 11022337 | tf_op jit(solution)/shard_map/while/body/eval_jaxpr/thk,khd->thd/dot_general | solution.py:38
  192.1 9.0 %convolution_convert_fusion = bf16[128,5120]{1,0:T(8,128)(2,1)} fusion(bf16[128,1536]{0,1:T(8,128)(2,1)S(1)} %bitcast.81, bf16[1536,5120]{1,0:T(8,128)(2,1)} %param.18), kind=kOutput, calls=%fused_computation.18 | convolution fusion | flops 2013921280 | bytes 17432576 | tf_op jit(solution)/shard_map/dot_general | solution.py:106
  204.7 34.6 %collective-permute-done.3 = bf16[256,1536]{0,1:T(8,128)(2,1)S(1)} collective-permute-done((bf16[256,1536]{0,1:T(8,128)(2,1)S(1)}, bf16[256,1536]{0,1:T(8,128)(2,1)S(1)}, u32[]{:S(2)}, u32[]{:S(2)}) %collective-permute-start.3) | collective-permute-done | bytes 786464 | tf_op jit(solution)/shard_map/ppermute | solution.py:15
  239.3 5.9 %concatenate.21 = bf16[1024,1536]{0,1:T(8,128)(2,1)} concatenate(bf16[32,1536]{0,1:T(8,128)(2,1)S(1)} %copy-done.2, bf16[32,1536]{0,1:T(8,128)(2,1)S(1)} %copy-done.4, bf16[64,1536]{0,1:T(8,128)(2,1)S(1)} %copy-done.6, bf16[128,1536]{0,1:T(8,128)(2,1)} %collective-permute-done.2, bf16[256,1536]{0,1:T(8,128)(2,1)S(1)} %collective-permute-done.3, bf16[32,1536]{0,1:T(8,128)(2,1)S(1)} %copy-done.2, ...), dimensions={0} | concatenate | bytes 6291456 | tf_op jit(solution)/shard_map/jit(_roll_dynamic)/concatenate | solution.py:19
  245.2 2.2 constant_dynamic-slice_fusion.2
  249.2 2.6 copy.32
  251.8 2.3 fusion.31
  255.1 2.3 add_convert_fusion
  (63 shorter events, 12.2 us)
Async XLA Ops:
  7.2 18.1 %copy-start.7 = (bf16[128,1536]{1,0:T(8,128)(2,1)S(1)}, bf16[128,1536]{1,0:T(8,128)(2,1)}, u32[]{:S(2)}) copy-start(bf16[128,1536]{1,0:T(8,128)(2,1)} %param.12) | copy-start | bytes 1179652
  7.2 86.6 %all-gather.4.cloned.1.call-start = ((), (), s32[]{:S(2)}) async-start(), calls=%async_computation.1 | async-start | bytes 6684672 | tf_op jit(solution)/shard_map/all_gather | solution.py:91
  9.2 151.2 %all-gather.6.cloned.1.call-start = ((), (), s32[]{:S(2)}) async-start(), calls=%async_computation.2 | async-start | bytes 6684672 | tf_op jit(solution)/shard_map/all_gather | solution.py:92
  11.2 238.0 %all-gather.8.cloned.1.call-start = ((), (), s32[]{:S(2)}) async-start(), calls=%async_computation.4 | async-start | bytes 1671168 | tf_op jit(solution)/shard_map/all_gather | solution.py:100
  12.4 148.0 %copy-start.1 = (bf16[32,1536]{0,1:T(8,128)(2,1)}, bf16[32,1536]{0,1:T(8,128)(2,1)S(1)}, u32[]{:S(2)}) copy-start(bf16[32,1536]{0,1:T(8,128)(2,1)S(1)} %copy.27) | copy-start | bytes 294916
  12.4 12.5 %collective-permute-start = (bf16[32,1536]{0,1:T(8,128)(2,1)S(1)}, bf16[32,1536]{0,1:T(8,128)(2,1)S(1)}, u32[]{:S(2)}, u32[]{:S(2)}) collective-permute-start(bf16[32,1536]{0,1:T(8,128)(2,1)S(1)} %copy.27), channel_id=1, source_target_pairs={{0,30},{2,0},{4,2},{6,4},{8,6},{10,8},{12,10},{14,12},{16,14},{18,... | collective-permute-start | bytes 294920 | tf_op jit(solution)/shard_map/ppermute | solution.py:15
  24.9 135.5 %copy-start.3 = (bf16[32,1536]{0,1:T(8,128)(2,1)}, bf16[32,1536]{0,1:T(8,128)(2,1)S(1)}, u32[]{:S(2)}) copy-start(bf16[32,1536]{0,1:T(8,128)(2,1)S(1)} %collective-permute-done) | copy-start | bytes 294916
  25.1 11.7 %collective-permute-start.1 = (bf16[64,1536]{0,1:T(8,128)(2,1)S(1)}, bf16[64,1536]{0,1:T(8,128)(2,1)S(1)}, u32[]{:S(2)}, u32[]{:S(2)}) collective-permute-start(bf16[64,1536]{0,1:T(8,128)(2,1)S(1)} %pad_maximum_fusion.1), channel_id=1, source_target_pairs={{0,28},{2,30},{4,0},{6,2},{8,4},{10,6},{12,8},{14,10},{16,12},{18,... | collective-permute-start | bytes 589832 | tf_op jit(solution)/shard_map/ppermute | solution.py:15
  25.2 229.9 %reduce-scatter.2.cloned.1.call-start = ((), (), s32[]{:S(2)}) async-start(), calls=%async_computation.3 | async-start | bytes 1966080 | tf_op jit(solution)/shard_map/reduce_scatter | solution.py:107
  36.8 123.6 %copy-start.5 = (bf16[64,1536]{0,1:T(8,128)(2,1)}, bf16[64,1536]{0,1:T(8,128)(2,1)S(1)}, u32[]{:S(2)}) copy-start(bf16[64,1536]{0,1:T(8,128)(2,1)S(1)} %collective-permute-done.1) | copy-start | bytes 589828
  37.9 163.2 %collective-permute-start.2 = (bf16[128,1536]{0,1:T(8,128)(2,1)}, bf16[128,1536]{0,1:T(8,128)(2,1)}, u32[]{:S(2)}, u32[]{:S(2)}) collective-permute-start(bf16[128,1536]{0,1:T(8,128)(2,1)} %pad_maximum_fusion.2), channel_id=1, source_target_pairs={{0,24},{2,26},{4,28},{6,30},{8,0},{10,2},{12,4},{14,6},{16,8},{18,... | collective-permute-start | bytes 1179656 | tf_op jit(solution)/shard_map/ppermute | solution.py:15
  167.8 4.0 %copy-start.9 = (f32[128,12]{0,1:T(8,128)S(1)}, f32[128,12]{0,1:T(8,128)}, u32[]{:S(2)}) copy-start(f32[128,12]{0,1:T(8,128)} %get-tuple-element.256) | copy-start | bytes 18436 | tf_op jit(solution)/shard_map/while
  167.8 4.7 %copy-start = (f32[12,1024,128]{2,1,0:T(8,128)S(1)}, f32[12,1024,128]{2,1,0:T(8,128)}, u32[]{:S(2)}) copy-start(f32[12,1024,128]{2,1,0:T(8,128)} %get-tuple-element.239) | copy-start | bytes 18874372 | tf_op jit(solution)/shard_map/while
  171.8 3.1 %copy-start.10 = (f32[128,12]{0,1:T(8,128)}, f32[128,12]{0,1:T(8,128)S(1)}, u32[]{:S(2)}) copy-start(f32[128,12]{0,1:T(8,128)S(1)} %get-tuple-element.267) | copy-start | bytes 18436 | tf_op jit(solution)/shard_map/while
  182.4 4.0 %copy-start.9 = (f32[128,12]{0,1:T(8,128)S(1)}, f32[128,12]{0,1:T(8,128)}, u32[]{:S(2)}) copy-start(f32[128,12]{0,1:T(8,128)} %get-tuple-element.256) | copy-start | bytes 18436 | tf_op jit(solution)/shard_map/while
  182.4 4.8 %copy-start = (f32[12,1024,128]{2,1,0:T(8,128)S(1)}, f32[12,1024,128]{2,1,0:T(8,128)}, u32[]{:S(2)}) copy-start(f32[12,1024,128]{2,1,0:T(8,128)} %get-tuple-element.239) | copy-start | bytes 18874372 | tf_op jit(solution)/shard_map/while
  186.4 4.4 %copy-start.10 = (f32[128,12]{0,1:T(8,128)}, f32[128,12]{0,1:T(8,128)S(1)}, u32[]{:S(2)}) copy-start(f32[128,12]{0,1:T(8,128)S(1)} %get-tuple-element.267) | copy-start | bytes 18436 | tf_op jit(solution)/shard_map/while
  192.1 9.1 %copy-start.2 = (bf16[32,1536]{0,1:T(8,128)(2,1)S(1)}, bf16[32,1536]{0,1:T(8,128)(2,1)}, u32[]{:S(2)}) copy-start(bf16[32,1536]{0,1:T(8,128)(2,1)} %copy-done.1) | copy-start | bytes 294916
  192.1 9.1 %copy-start.4 = (bf16[32,1536]{0,1:T(8,128)(2,1)S(1)}, bf16[32,1536]{0,1:T(8,128)(2,1)}, u32[]{:S(2)}) copy-start(bf16[32,1536]{0,1:T(8,128)(2,1)} %copy-done.3) | copy-start | bytes 294916
  192.1 9.1 %copy-start.6 = (bf16[64,1536]{0,1:T(8,128)(2,1)S(1)}, bf16[64,1536]{0,1:T(8,128)(2,1)}, u32[]{:S(2)}) copy-start(bf16[64,1536]{0,1:T(8,128)(2,1)} %copy-done.5) | copy-start | bytes 589828
  201.1 3.4 %copy-start.8 = (bf16[128,1536]{1,0:T(8,128)(2,1)S(1)}, bf16[128,1536]{1,0:T(8,128)(2,1)}, u32[]{:S(2)}) copy-start(bf16[128,1536]{1,0:T(8,128)(2,1)} %param.15) | copy-start | bytes 1179652
  202.8 36.4 %collective-permute-start.3 = (bf16[256,1536]{0,1:T(8,128)(2,1)S(1)}, bf16[256,1536]{0,1:T(8,128)(2,1)S(1)}, u32[]{:S(2)}, u32[]{:S(2)}) collective-permute-start(bf16[256,1536]{0,1:T(8,128)(2,1)S(1)} %pad_maximum_fusion), channel_id=1, source_target_pairs={{0,16},{2,18},{4,20},{6,22},{8,24},{10,26},{12,28},{14,30},{16,0},... | collective-permute-start | bytes 2359304 | tf_op jit(solution)/shard_map/ppermute | solution.py:15
Sparse Core Ops, SparseCore 0:
  10.7 82.9 all-gather.3
  96.5 63.8 all-gather.5
  162.7 37.8 all-gather.7
  202.6 22.0 reduce-scatter.1
